TPU v7x, 256 devices: a whole 4x4x8 slice. The times are simulated.
256 devices in a mesh: row: 4 (over x_lo, core), col: 64 (over y, x_hi, z).
Axes of the slice: x: 4 (x_hi: 2, x_lo: 2; x = x_hi * 2 + x_lo), y: 4, z: 8, core: 2. Of those that a mesh axis runs over, the one named last changes fastest.
Arguments:
- test_points: float32 [3, 4096], P(None, ('row', 'col')), may hold values from 0 to 1
- src_points: float32 [3, 262144], P(None, ('row', 'col')), may hold values from 0 to 1
- currents: float32 [2, 262144], P(None, ('row', 'col')), may hold values from -6 to 6
- near_blocks: float32 [16384, 2, 16, 128], P(('row', 'col')), may hold values from -0.3 to 0.3
- near_dest: int32 [16384, 1], P(('row', 'col')), may hold values from 0 to 63; in each aligned block of 64 rows (0 to 63, 64 to 127, ...) at most 2 rows name the same one
- near_tile: int32 [16384, 1], P(('row', 'col')), may hold values from 0 to 7
Outputs:
- field: float32 [2, 4096], P(None, ('row', 'col'))
Inputs may be any that keep to these rules, and one draw needn't show every extreme that they name: `near_dest`: among the 64 blocks held by one device, at most 2 name the same column index; some device reaches 2 in every draw.
All inputs are finite; a program needn't handle non-finite values.
Results may differ from a plain program's by a relative error of at most 0.0003.
Values sent between devices are 32-bit elements; how exact they have to be, the bound alone decides.
A program may use at most 64 MiB of HBM per device.

v0:
```python
import math

import jax
import jax.numpy as jnp
from jax import lax
from jax.sharding import PartitionSpec as P

CAP = 2


WAVENUMBER = 40.0
SOFTENING = 0.01


def far_terms(targets, sources, current):
    row_count = targets.shape[1]
    src_width = sources.shape[1]
    entry_limit = max(128, (1 << 20) // row_count)
    stride = math.gcd(src_width, 1 << entry_limit.bit_length() - 1)
    blocks = src_width // stride
    source_blocks = sources.reshape(3, blocks, stride).transpose(1, 0, 2)
    current_blocks = current.reshape(2, blocks, stride).transpose(1, 0, 2)

    def accumulate(running, block_pair):
        points, values = block_pair
        delta_x = targets[0][:, None] - points[0][None, :]
        delta_y = targets[1][:, None] - points[1][None, :]
        delta_z = targets[2][:, None] - points[2][None, :]
        distance = jnp.sqrt(
            delta_x * delta_x + delta_y * delta_y + delta_z * delta_z + SOFTENING * SOFTENING
        )
        phases = WAVENUMBER * distance
        kernel_re = jnp.cos(phases) / distance
        kernel_im = -jnp.sin(phases) / distance
        real_part = jnp.sum(kernel_re * values[0][None, :] - kernel_im * values[1][None, :], axis=1)
        imag_part = jnp.sum(kernel_re * values[1][None, :] + kernel_im * values[0][None, :], axis=1)
        return (running + jnp.stack([real_part, imag_part]), None)

    running, _ = lax.scan(
        accumulate, jnp.zeros((2, row_count), jnp.float32), (source_blocks, current_blocks)
    )
    return running


def far_part(test_points, src_points, currents):
    block_src, block_cur = (
        lax.all_gather(src_points, "row", axis=1, tiled=True),
        lax.all_gather(currents, "row", axis=1, tiled=True),
    )
    return far_terms(
        test_points,
        lax.all_gather(block_src, "col", axis=1, tiled=True),
        lax.all_gather(block_cur, "col", axis=1, tiled=True),
    )


def near_part(currents, near_blocks, near_dest, near_tile):
    items = near_blocks.shape[0]
    row_dev = near_blocks.shape[2]
    tile_width = near_blocks.shape[3]
    columns = lax.axis_size("col")
    tile_count = currents.shape[1] // tile_width
    highest = lax.Precision.HIGHEST
    tile_ids = near_tile[:, 0]
    target_col = near_dest[:, 0]
    picker = (tile_ids[:, None] == jnp.arange(tile_count, dtype=jnp.int32)[None, :]).astype(
        jnp.float32
    )
    chosen = jnp.einsum(
        "kt,ctj->kcj", picker, currents.reshape(2, tile_count, tile_width), precision=highest
    )
    blocks_re = near_blocks[:, 0]
    blocks_im = near_blocks[:, 1]
    term_re = jnp.einsum("kij,kj->ki", blocks_re, chosen[:, 0], precision=highest) - jnp.einsum(
        "kij,kj->ki", blocks_im, chosen[:, 1], precision=highest
    )
    term_im = jnp.einsum("kij,kj->ki", blocks_re, chosen[:, 1], precision=highest) + jnp.einsum(
        "kij,kj->ki", blocks_im, chosen[:, 0], precision=highest
    )
    terms = jnp.concatenate([term_re, term_im], axis=1)
    positions = jnp.arange(items, dtype=jnp.int32)
    earlier = (target_col[:, None] == target_col[None, :]) & (
        positions[None, :] < positions[:, None]
    )
    ranking = jnp.sum(earlier.astype(jnp.int32), axis=1)
    slot_ids = target_col * CAP + ranking
    placer = (slot_ids[:, None] == jnp.arange(columns * CAP, dtype=jnp.int32)[None, :]).astype(
        jnp.float32
    )
    outgoing = jnp.einsum("ks,kf->sf", placer, terms, precision=highest).reshape(
        columns, CAP * 2 * row_dev
    )
    incoming = lax.all_to_all(outgoing, "col", split_axis=0, concat_axis=0, tiled=True)
    return incoming.reshape(columns * CAP, 2, row_dev).sum(axis=0)


def local(test_points, src_points, currents, near_blocks, near_dest, near_tile):
    total_sources = src_points.shape[1] * lax.axis_size("row") * lax.axis_size("col")
    factor = 1.0 / math.sqrt(total_sources)
    far = far_part(test_points, src_points, currents)
    near = near_part(currents, near_blocks, near_dest, near_tile)
    return far * factor + near


def solution(mesh):
    in_specs = (
        P(None, ("row", "col")),
        P(None, ("row", "col")),
        P(None, ("row", "col")),
        P(("row", "col"), None, None, None),
        P(("row", "col"), None),
        P(("row", "col"), None),
    )
    out_specs = P(None, ("row", "col"))
    return jax.shard_map(local, mesh=mesh, in_specs=in_specs, out_specs=out_specs, check_vma=False)
```

profile of v0, /device:TPU:1, one launch (start us, length us, event | category | flops | bytes accessed | tf_op | source)
XLA Modules:
  0.0 360.9 jit_solution(17013263100812028713)
XLA Ops:
  6.5 8.9 %all_gather.14 = f32[2,4096]{1,0:T(2,128)} all-gather(f32[2,1024]{1,0:T(2,128)} %param.10), channel_id=1, replica_groups=mesh['row'=4,'col'=64] {'row'}, dimensions={1}, use_global_device_ids=true | all-gather | bytes 40960 | tf_op jit(solution)/shard_map/all_gather | solution.py:48
  15.5 6.5 %all_gather.12 = f32[3,4096]{1,0:T(4,128)} all-gather(f32[3,1024]{1,0:T(4,128)} %param.9), channel_id=1, replica_groups=mesh['row'=4,'col'=64] {'row'}, dimensions={1}, use_global_device_ids=true | all-gather | bytes 61440 | tf_op jit(solution)/shard_map/all_gather | solution.py:47
  22.0 0.9 fusion.18
  22.9 2.0 fusion.6
  24.9 2.0 fusion.2
  26.9 2.0 fusion.4
  28.9 2.0 fusion
  30.9 0.9 convert_reduce_fusion
  33.5 12.6 %all-to-all-start = ((f32[64,1,64]{2,1,0:T(1,128)}), f32[64,1,64]{2,1,0:T(1,128)S(1)}, u32[]{:S(2)}, u32[]{:S(2)}) async-start(f32[64,1,64]{2,1,0:T(1,128)} %bitcast.27), calls=%async_computation | async-start | bytes 65536 | tf_op jit(solution)/shard_map/all_to_all | solution.py:93
  46.1 10.8 %all-to-all-done = f32[64,1,64]{2,1,0:T(1,128)S(1)} async-done(((f32[64,1,64]{2,1,0:T(1,128)}), f32[64,1,64]{2,1,0:T(1,128)S(1)}, u32[]{:S(2)}, u32[]{:S(2)}) %all-to-all-start) | async-done | bytes 16416 | tf_op jit(solution)/shard_map/all_to_all | solution.py:93
  58.4 73.2 %all-gather.5.cloned.1.call-done = f32[2,262144]{1,0:T(2,128)} async-done(((f32[2,4096]{1,0:T(2,128)}), f32[2,262144]{1,0:T(2,128)}) %all-gather.5.cloned.1.call-update) | async-done | bytes 2097168 | tf_op jit(solution)/shard_map/all_gather | solution.py:53
  131.6 128.0 %all-gather.3.cloned.1.call-done = f32[3,262144]{1,0:T(4,128)} async-done(((f32[3,4096]{1,0:T(4,128)}), f32[3,262144]{1,0:T(4,128)}) %all-gather.3.cloned.1.call-update) | async-done | bytes 3145744 | tf_op jit(solution)/shard_map/all_gather | solution.py:52
  259.7 93.8 %while.11 = (s32[]{:T(128)}, f32[2,16]{1,0:T(2,128)S(1)}, f32[3,16]{1,0:T(4,128)}, f32[4,3,65536]{2,1,0:T(4,128)}, f32[4,2,65536]{2,1,0:T(2,128)}, /*index=5*/s32[]{:T(128)}, s32[]{:T(128)}, s32[]{}, s32[]{}) while((s32[]{:T(128)}, f32[2,16]{1,0:T(2,128)S(1)}, f32[3,16]{1,0:T(4,128)}, f32[4,3,65536]{2,1,0:T(4,128)}, ...), condition=%wide.region_3.4_spmd.clone, body=%wide.region_0.3_spmd.clone.sunk | while | flops 22020164 | bytes 3933387 | solution.py:39
  259.7 3.4 constant_dynamic-slice_fusion.6
  263.1 0.8 slice_bitcast_fusion.4
  263.9 19.1 %subtract_reduce_fusion.2 = (f32[16]{0:T(128)S(1)}, f32[16]{0:T(128)S(1)}) fusion(f32[65536]{0:T(1024)S(1)} %bitcast.82, f32[65536]{0:T(1024)S(1)} %bitcast.81, f32[65536]{0:T(1024)S(1)} %bitcast.83, f32[16]{0:T(128)S(1)} %get-tuple-element.120, f32[65536]{0:T(1024)S(1)} %bitcast.84, f32[16]{0:T(128)S(1)} %get-tuple-element.122, ...), kind=kLoop, calls=%fused_computation.1.clone.1 | loop fusion | flops 22020064 | bytes 1311040 | tf_op jit(solution)/shard_map/while/body/eval_jaxpr/reduce_sum | solution.py:35
  283.0 3.7 %constant_dynamic-slice_fusion.6 = (f32[1,1,65536]{2,1,0:T(1,128)S(1)}, f32[1,1,65536]{2,1,0:T(1,128)S(1)}, f32[1,1,65536]{2,1,0:T(1,128)S(1)}, f32[1,1,65536]{2,1,0:T(1,128)S(1)}, f32[1,1,65536]{2,1,0:T(1,128)S(1)}) fusion(f32[4,2,65536]{2,1,0:T(2,128)} %get-tuple-element.149, s32[]{:T(128)} %get-tuple-element.136, s32[]{:T(128)S(6)} %add.101, ...), kind=kLoop, calls=%fused_computation.5.clone.1 | loop fusion | bytes 2621452 | tf_op jit(solution)/shard_map/while/body/eval_jaxpr/slice | solution.py:35
  286.7 0.8 slice_bitcast_fusion.4
  287.5 19.1 %subtract_reduce_fusion.2 = (f32[16]{0:T(128)S(1)}, f32[16]{0:T(128)S(1)}) fusion(f32[65536]{0:T(1024)S(1)} %bitcast.82, f32[65536]{0:T(1024)S(1)} %bitcast.81, f32[65536]{0:T(1024)S(1)} %bitcast.83, f32[16]{0:T(128)S(1)} %get-tuple-element.120, f32[65536]{0:T(1024)S(1)} %bitcast.84, f32[16]{0:T(128)S(1)} %get-tuple-element.122, ...), kind=kLoop, calls=%fused_computation.1.clone.1 | loop fusion | flops 22020064 | bytes 1311040 | tf_op jit(solution)/shard_map/while/body/eval_jaxpr/reduce_sum | solution.py:35
  306.6 3.5 constant_dynamic-slice_fusion.6
  310.1 0.8 slice_bitcast_fusion.4
  310.9 19.1 %subtract_reduce_fusion.2 = (f32[16]{0:T(128)S(1)}, f32[16]{0:T(128)S(1)}) fusion(f32[65536]{0:T(1024)S(1)} %bitcast.82, f32[65536]{0:T(1024)S(1)} %bitcast.81, f32[65536]{0:T(1024)S(1)} %bitcast.83, f32[16]{0:T(128)S(1)} %get-tuple-element.120, f32[65536]{0:T(1024)S(1)} %bitcast.84, f32[16]{0:T(128)S(1)} %get-tuple-element.122, ...), kind=kLoop, calls=%fused_computation.1.clone.1 | loop fusion | flops 22020064 | bytes 1311040 | tf_op jit(solution)/shard_map/while/body/eval_jaxpr/reduce_sum | solution.py:35
  330.0 3.6 constant_dynamic-slice_fusion.6
  334.4 19.1 %subtract_reduce_fusion.2 = (f32[16]{0:T(128)S(1)}, f32[16]{0:T(128)S(1)}) fusion(f32[65536]{0:T(1024)S(1)} %bitcast.82, f32[65536]{0:T(1024)S(1)} %bitcast.81, f32[65536]{0:T(1024)S(1)} %bitcast.83, f32[16]{0:T(128)S(1)} %get-tuple-element.120, f32[65536]{0:T(1024)S(1)} %bitcast.84, f32[16]{0:T(128)S(1)} %get-tuple-element.122, ...), kind=kLoop, calls=%fused_computation.1.clone.1 | loop fusion | flops 22020064 | bytes 1311040 | tf_op jit(solution)/shard_map/while/body/eval_jaxpr/reduce_sum | solution.py:35
  (21 shorter events, 4.7 us)
Async XLA Ops:
  6.5 125.1 %all-gather.5.cloned.1.call-start = ((), (), s32[]{:S(2)}) async-start(), calls=%async_computation.2 | async-start | bytes 2129920 | tf_op jit(solution)/shard_map/all_gather | solution.py:53
  15.4 244.3 %all-gather.3.cloned.1.call-start = ((), (), s32[]{:S(2)}) async-start(), calls=%async_computation.1 | async-start | bytes 4259840 | tf_op jit(solution)/shard_map/all_gather | solution.py:52
  33.5 23.4 %all-to-all-start = ((f32[64,1,64]{2,1,0:T(1,128)}), f32[64,1,64]{2,1,0:T(1,128)S(1)}, u32[]{:S(2)}, u32[]{:S(2)}) async-start(f32[64,1,64]{2,1,0:T(1,128)} %bitcast.27), calls=%async_computation | async-start | bytes 65536 | tf_op jit(solution)/shard_map/all_to_all | solution.py:93
Sparse Core Ops, SparseCore 0:
  15.5 116.0 all-gather.4
  135.2 124.4 all-gather.2
where the time goes:
time: 364 us; the launch traced here: 361 us
  waiting for transfers between devices  212 us (58%)
  other arithmetic  79.4 us (22%)
  local copies, waits for them, and re-layouts  18.7 us (5%)
  blocking collectives  15.3 us (4%)
  between operations  13.5 us (4%)
  starting transfers between devices  12.6 us (3%)
  matrix products  9.21 us (3%)
    all_gather x1, waiting for transfers between devices, far_part(): lax.all_gather(block_src, 'col', axis=1, tiled=True)  128 us
    reduce_sum x4, other arithmetic, accumulate(): jnp.sum(kernel_re * values[0][None, :] - kernel_im * values[1][None, :],...  76.3 us
    all_gather x1, waiting for transfers between devices, far_part(): lax.all_gather(block_cur, 'col', axis=1, tiled=True)  73.2 us
    slice x4, local copies, waits for them, and re-layouts, accumulate(): values[0][None, :]  14.1 us
    all_to_all x1, starting transfers between devices, near_part(): lax.all_to_all(outgoing, 'col', split_axis=0, concat_axis=0, tiled=True)  12.6 us
    all_to_all x1, waiting for transfers between devices, near_part(): lax.all_to_all(outgoing, 'col', split_axis=0, concat_axis=0, tiled=True)  10.8 us
    all_gather x1, blocking collectives, far_part(): lax.all_gather(currents, 'row', axis=1, tiled=True)  8.85 us
  transfers between devices with their start and end apart: 3, of which 3 were waited for; matrix products, arithmetic and copies ran while one was open for 3% of the time, Pallas kernels for 0%

commit v1 on v0

v1 whole, which is shorter than its diff:
```python
import functools
import math

import jax
import jax.numpy as jnp
from jax import lax
from jax.experimental import pallas as pl
from jax.experimental.pallas import tpu as pltpu
from jax.sharding import PartitionSpec as P

F32, BF16 = jnp.float32, jnp.bfloat16
MESH = pl.DeviceIdType.MESH
WAVENUMBER = 40.0
SOFTENING = 0.01
TURNS = WAVENUMBER / (2.0 * math.pi)
EPS2 = (TURNS * SOFTENING) ** 2
S0, S1, S2, S3 = 3.141557035259913, -5.166470369169727, 2.537091227972406, -0.544489261808413
B0, B1, B2 = S0 / S3, S1 / S3, S2 / S3
ONE = (1.0 + 4e-7) / S3**2
CHUNK = 128
LANES = 128
FEATURES = 80
ATAN = (0.9999998864, -0.3333259702, 0.1998590671, -0.1416122883, 0.1049894485, -0.07234855029, 0.03978119812, -0.01440134322, 0.002456721093)


def two(x):
    scaled = x * 65537.0
    high = scaled - (scaled - x)
    return high, x - high


def rows(base, *pairs):
    index = lax.broadcasted_iota(jnp.int32, base.shape, 0)
    for row, value in pairs:
        base = jnp.where(index == row, value, base)
    return base


def pieces(points, extra):
    coarse = jnp.round(points * 32.0) * (1.0 / 32.0)
    rest = points - coarse
    middle, rest2 = two(rest)
    fine, _ = two(rest2)
    grid = jnp.sum(coarse * coarse, axis=0, keepdims=True)
    off = jnp.sum(rest * (points + coarse), axis=0, keepdims=True) + extra
    g1, g2 = two(grid)
    o1, left = two(off)
    o2, o3 = two(left)
    return coarse, middle, fine, g1, g2, o1, o2, o3


def source_features(packed):
    points = rows(packed, *[(r, 0.0) for r in range(3, 8)])
    coarse, middle, fine, g1, g2, o1, o2, o3 = pieces(points, EPS2)
    a1, left = two(packed[4:5])
    a2, a3 = two(left)
    w1, left = two(packed[3:4])
    w2, w3 = two(left)
    zero = jnp.zeros_like(coarse)
    return [
        rows(coarse, (3, g1), (4, g2), (5, 1.0), (6, 1.0)),
        rows(coarse, (3, o1), (4, o2), (5, o3), (6, 1.0), (7, 1.0)),
        rows(coarse, (3, 1.0)),
        middle,
        fine,
        middle,
        middle,
        fine,
        rows(zero, (0, a1), (1, a2), (2, a3), (3, w1), (4, w2), (5, w3)),
        zero,
    ]


def target_features(points):
    coarse, middle, fine, g1, g2, o1, o2, o3 = pieces(points, 0.0)
    coarse, middle, fine = -2.0 * coarse, -2.0 * middle, -2.0 * fine
    zero = jnp.zeros_like(coarse)
    return [
        rows(coarse, (3, 1.0), (4, 1.0), (5, g1), (6, g2)),
        rows(middle, (3, 1.0), (4, 1.0), (5, 1.0), (6, o1), (7, o2)),
        rows(fine, (3, o3)),
        coarse,
        coarse,
        middle,
        fine,
        middle,
        zero,
        zero,
    ]


def pair_sums(q, shift, weight, sums):
    total, cosines, sines = sums
    inverse = lax.rsqrt(q)
    turns = q * inverse - shift
    part = turns - jnp.round(turns)
    z = part * part
    sine = part * (((z + B2) * z + B1) * z + B0)
    rest = ONE - sine * sine
    w = weight * inverse
    g = w * rest
    return total + w, cosines + g, sines + g * (sine * lax.rsqrt(rest))


def polar(re, im):
    are, aim = jnp.abs(re), jnp.abs(im)
    big, small = jnp.maximum(are, aim), jnp.minimum(are, aim)
    ratio = small / jnp.where(big > 0.0, big, 1.0)
    square = ratio * ratio
    angle = ATAN[-1]
    for c in ATAN[-2::-1]:
        angle = angle * square + c
    angle = angle * ratio * (0.5 / math.pi)
    angle = jnp.where(aim > are, 0.25 - angle, angle)
    angle = jnp.where(re < 0.0, 0.5 - angle, angle)
    return big * jnp.sqrt(1.0 + square), jnp.where(im < 0.0, -angle, angle)


def dot(a, b, ca, cb):
    return lax.dot_general(a.astype(BF16), b.astype(BF16), (((ca,), (cb,)), ((), ())), preferred_element_type=F32)


def near_rows(currents, blocks, dest, tile, planes):
    items, _, width, depth = blocks.shape
    tiles = currents.shape[1] // depth
    cur = jnp.concatenate(
        [currents[c : c + 1, t * depth : (t + 1) * depth] for c in range(2) for t in range(tiles)], axis=0
    )
    ch, cl = two(cur)
    both = jnp.concatenate([ch, cl], axis=0)
    n = items * width

    def against(part):
        bh, bl = two(blocks[:, part].reshape(n, depth))
        high = dot(both, bh, 1, 1)
        return high[: 2 * tiles] + high[2 * tiles :] + dot(ch, bl, 1, 1)

    ur, ui = against(0), against(1)
    real = ur[:tiles] - ui[tiles:]
    imag = ur[tiles:] + ui[:tiles]
    spread = (
        lax.broadcasted_iota(jnp.int32, (items, n), 1) // width == lax.broadcasted_iota(jnp.int32, (items, n), 0)
    ).astype(F32)
    along = lambda v, k: dot(jnp.broadcast_to(v.astype(F32), (items, k)), spread, 0, 0)
    mine = along(tile, tiles) == lax.broadcasted_iota(jnp.int32, (tiles, n), 0).astype(F32)
    real = jnp.sum(jnp.where(mine, real, 0.0), axis=0, keepdims=True)
    imag = jnp.sum(jnp.where(mine, imag, 0.0), axis=0, keepdims=True)
    plane = along(dest % planes, planes) == lax.broadcasted_iota(jnp.int32, (planes, n), 0).astype(F32)
    left = jnp.concatenate([jnp.where(plane, real, 0.0), jnp.where(plane, imag, 0.0)], axis=0)
    place = dot(spread, jnp.broadcast_to((dest // planes).astype(F32), (items, LANES)), 0, 0)
    lane = lax.broadcasted_iota(jnp.int32, (n, LANES), 1)
    row = lax.broadcasted_iota(jnp.int32, (n, LANES), 0)
    right = jnp.where((lane % width == row % width) & (place == (lane // width).astype(F32)), 1.0, 0.0)
    l1, rest = two(left)
    l2, l3 = two(rest)
    k = 2 * planes
    out = dot(jnp.concatenate([l1, l2, l3], axis=0), right, 1, 0)
    return out[:k] + out[k : 2 * k] + out[2 * k :]


def kernel(
    n_row, n_col, planes, scale,
    tp_ref, src_ref, cur_ref, blocks_hbm, dest_ref, tile_ref, out_ref,
    tbuf, sbuf, nbuf, nsend, rbuf, rsend, blocks, fa, fb, q_ref,
    copy_sem, tsend_sem, trecv_sem, ssend_sem, srecv_sem, nsend_sem, nrecv_sem, rsend_sem, rrecv_sem,
):
    places = n_col // planes
    members = n_row * places
    width = tp_ref.shape[1]
    n_src = src_ref.shape[1]
    n_tgt = n_row * LANES
    row, col = lax.axis_index("row"), lax.axis_index("col")
    place, plane = col // planes, col % planes
    me = row * places + place

    fetch = pltpu.make_async_copy(blocks_hbm, blocks, copy_sem)
    fetch.start()

    def member(k):
        other = lax.rem(me + k, members)
        return other, (other // places, lax.rem(other, places) * planes + plane)

    def level(k):
        other = lax.rem(plane + k, planes)
        return other, (row, place * planes + other)

    barrier = pltpu.get_barrier_semaphore()

    def greet(k, _):
        pl.semaphore_signal(barrier, inc=1, device_id=member(k)[1], device_id_type=MESH)
        return 0

    def greet_level(k, _):
        pl.semaphore_signal(barrier, inc=1, device_id=level(k)[1], device_id_type=MESH)
        return 0

    lax.fori_loop(1, planes, greet_level, 0)
    lax.fori_loop(1, members, greet, 0)

    points = (tp_ref[...] - 0.5) * TURNS
    repeated = jnp.concatenate([points] * (LANES // width), axis=1)
    lane = lax.broadcasted_iota(jnp.int32, repeated.shape, 1)
    tbuf[me] = jnp.concatenate(
        [jnp.where(lane // width == place, repeated, 0.0), jnp.zeros((1, LANES), F32)], axis=0
    )
    size, angle = polar(cur_ref[0:1, :], cur_ref[1:2, :])
    sbuf[plane] = jnp.concatenate(
        [(src_ref[...] - 0.5) * TURNS, size, angle, jnp.zeros((3, n_src), F32)], axis=0
    )

    for i in range(FEATURES // 8):
        fb[pl.ds(i * 8, 8), :] = jnp.zeros((8, n_tgt + 2 * LANES), BF16)
    index = lax.broadcasted_iota(jnp.int32, (16, LANES), 0)
    fb[pl.ds(64, 16), pl.ds(n_tgt, LANES)] = jnp.where(index < 3, 1.0, 0.0).astype(BF16)
    fb[pl.ds(64, 16), pl.ds(n_tgt + LANES, LANES)] = jnp.where((index >= 3) & (index < 6), 1.0, 0.0).astype(BF16)

    def prepare(which, slot):
        groups = source_features(sbuf[which])
        for i in range(0, len(groups), 2):
            fa[slot, pl.ds(i * 8, 16), :] = jnp.concatenate(groups[i : i + 2], axis=0).astype(BF16)

    prepare(plane, 0)

    fetch.wait()
    near = near_rows(cur_ref[...], blocks, dest_ref[...], tile_ref[...], planes)
    for k in range(planes):
        nsend[k] = jnp.concatenate([near[k : k + 1], near[planes + k : planes + k + 1]], axis=0)

    pl.semaphore_wait(barrier, members - 1 + planes - 1)

    def target_copy(k):
        other, device = member(k)
        return other, lambda slot, sem: pltpu.make_async_remote_copy(
            src_ref=tbuf.at[slot], dst_ref=tbuf.at[slot], send_sem=tsend_sem.at[other],
            recv_sem=trecv_sem.at[sem], device_id=device, device_id_type=MESH,
        )

    def source_copy(k):
        other, device = level(k)
        return other, lambda slot, sem: pltpu.make_async_remote_copy(
            src_ref=sbuf.at[slot], dst_ref=sbuf.at[slot], send_sem=ssend_sem.at[other],
            recv_sem=srecv_sem.at[sem], device_id=device, device_id_type=MESH,
        )

    def near_copy(k):
        other, device = level(k)
        return other, lambda slot, sem: pltpu.make_async_remote_copy(
            src_ref=nsend.at[other], dst_ref=nbuf.at[slot], send_sem=nsend_sem.at[other],
            recv_sem=nrecv_sem.at[sem], device_id=device, device_id_type=MESH,
        )

    def result_copy(k):
        other, device = member(k)
        return other, lambda slot, sem: pltpu.make_async_remote_copy(
            src_ref=rsend.at[other // places], dst_ref=rbuf.at[slot], send_sem=rsend_sem.at[other],
            recv_sem=rrecv_sem.at[sem], device_id=device, device_id_type=MESH,
        )

    def each(copy, count, mine, act):
        def body(k, _):
            other, make = copy(k)
            if act == "start":
                make(mine, mine).start()
            elif act == "recv":
                make(other, other).wait_recv()
            else:
                make(mine, mine).wait_send()
            return 0

        lax.fori_loop(1, count, body, 0)

    def offset(i):
        half = (i + 1) // 2
        return lax.rem(planes + (2 * lax.rem(i, 2) - 1) * half, planes)

    each(target_copy, members, me, "start")

    def send_source(i, _):
        _, make = source_copy(offset(i))
        make(plane, plane).start()
        return 0

    lax.fori_loop(1, planes, send_source, 0)
    nbuf[plane] = nsend[plane]
    each(near_copy, planes, plane, "start")

    each(target_copy, members, me, "recv")
    points = []
    for g in range(n_row):
        joined = tbuf[g * places]
        for s in range(1, places):
            joined = joined + tbuf[g * places + s]
        points.append(joined)
    points = jnp.concatenate(points, axis=1)
    points = jnp.concatenate([points, jnp.zeros((4, n_tgt), F32)], axis=0)
    groups = target_features(points)
    for i in range(0, len(groups), 2):
        fb[pl.ds(i * 8, 16), pl.ds(0, n_tgt)] = jnp.concatenate(groups[i : i + 2], axis=0).astype(BF16)

    chunks = n_src // CHUNK

    def distances(slot, chunk, into):
        part = fa[slot, :, pl.ds(chunk * CHUNK, CHUNK)]
        q_ref[into] = lax.dot_general(part, fb[...], (((0,), (0,)), ((), ())), preferred_element_type=F32)

    def add_up(chunk, sums):
        for r in range(CHUNK // 8):
            q = q_ref[chunk, pl.ds(r * 8, 8), pl.ds(0, n_tgt)]
            shift = q_ref[chunk, pl.ds(r * 8, 8), pl.ds(n_tgt, LANES)]
            weight = q_ref[chunk, pl.ds(r * 8, 8), pl.ds(n_tgt + LANES, LANES)]
            sums = pair_sums(q, jnp.tile(shift, (1, n_row)), jnp.tile(weight, (1, n_row)), sums)
        return sums

    distances(0, 0, 0)

    def block(i, sums):
        ahead = jnp.minimum(i + 1, planes - 1)

        @pl.when(i < planes - 1)
        def _():
            other, make = source_copy(offset(ahead))
            make(other, other).wait_recv()

        slot = lax.rem(i, 2)
        prepare(lax.rem(plane + offset(ahead), planes), 1 - slot)
        for c in range(chunks):
            if c < chunks - 1:
                distances(slot, c + 1, c + 1)
            else:
                distances(1 - slot, 0, 0)
            sums = add_up(c, sums)
        return sums

    zero = jnp.zeros((8, n_tgt), F32)
    total, cosines, sines = lax.fori_loop(0, planes, block, (zero, zero, zero))
    unit = scale * TURNS
    real = jnp.sum((2.0 * S3 * S3) * cosines - total, axis=0, keepdims=True) * unit
    imag = jnp.sum(sines, axis=0, keepdims=True) * (-2.0 * S3 * abs(S3) * unit)

    each(near_copy, planes, plane, "recv")
    near = nbuf[0]
    for k in range(1, planes):
        near = near + nbuf[k]
    for g in range(n_row):
        part = jnp.concatenate([real[:, g * LANES : (g + 1) * LANES], imag[:, g * LANES : (g + 1) * LANES]], axis=0)
        part = part + jnp.where(row == g, 1.0, 0.0) * near
        rsend[g] = part
    rbuf[me] = rsend[row]
    each(result_copy, members, me, "start")
    each(target_copy, members, me, "send")
    each(source_copy, planes, plane, "send")
    each(near_copy, planes, plane, "send")
    each(result_copy, members, me, "recv")
    field = rbuf[0]
    for k in range(1, members):
        field = field + rbuf[k]
    field = jnp.concatenate([field, jnp.zeros((6, LANES), F32)], axis=0)
    field = pltpu.roll(field, lax.rem(LANES - place * width, LANES), 1)
    out_ref[...] = field[0:2, 0:width]
    each(result_copy, members, me, "send")


def local(planes, total_sources, test_points, src_points, currents, near_blocks, near_dest, near_tile):
    n_row, n_col = lax.axis_size("row"), lax.axis_size("col")
    members = n_row * (n_col // planes)
    n_src = src_points.shape[1]
    n_tgt = n_row * LANES
    vmem = pl.BlockSpec(memory_space=pltpu.VMEM)
    dma = pltpu.SemaphoreType.DMA
    return pl.pallas_call(
        functools.partial(kernel, n_row, n_col, planes, 1.0 / math.sqrt(total_sources)),
        out_shape=jax.ShapeDtypeStruct((2, test_points.shape[1]), F32),
        in_specs=[vmem, vmem, vmem, pl.BlockSpec(memory_space=pl.ANY), vmem, vmem],
        out_specs=vmem,
        scratch_shapes=[
            pltpu.VMEM((members, 4, LANES), F32),
            pltpu.VMEM((planes, 8, n_src), F32),
            pltpu.VMEM((planes, 2, LANES), F32),
            pltpu.VMEM((planes, 2, LANES), F32),
            pltpu.VMEM((members, 2, LANES), F32),
            pltpu.VMEM((n_row, 2, LANES), F32),
            pltpu.VMEM(near_blocks.shape, F32),
            pltpu.VMEM((2, FEATURES, n_src), BF16),
            pltpu.VMEM((FEATURES, n_tgt + 2 * LANES), BF16),
            pltpu.VMEM((n_src // CHUNK, CHUNK, n_tgt + 2 * LANES), F32),
            dma,
            dma((members,)),
            dma((members,)),
            dma((planes,)),
            dma((planes,)),
            dma((planes,)),
            dma((planes,)),
            dma((members,)),
            dma((members,)),
        ],
        compiler_params=pltpu.CompilerParams(collective_id=0, has_side_effects=True, vmem_limit_bytes=48 << 20),
    )(test_points, src_points, currents, near_blocks, near_dest, near_tile)


def solution(mesh):
    planes = min(8, mesh.shape["col"])

    def whole(test_points, src_points, currents, near_blocks, near_dest, near_tile):
        both = ("row", "col")
        return jax.shard_map(
            functools.partial(local, planes, src_points.shape[1]),
            mesh=mesh,
            in_specs=(
                P(None, both), P(None, both), P(None, both), P(both, None, None, None), P(both, None), P(both, None),
            ),
            out_specs=P(None, both),
            check_vma=False,
        )(test_points, src_points, currents, near_blocks, near_dest, near_tile)

    return whole
```

time: 364 us -> 41.2 us (0.11)
  waiting for transfers between devices: 212 us -> 0 us
  other arithmetic: 79.4 us -> 0 us
  Pallas kernels: 0 us -> 37.7 us
  local copies, waits for them, and re-layouts: 18.7 us -> 3.25 us
  blocking collectives: 15.3 us -> 0 us
  between operations: 13.5 us -> 0.04 us
  starting transfers between devices: 12.6 us -> 0 us
  matrix products: 9.21 us -> 0 us
    all_gather x2 -> x0, waiting for transfers between devices: 201 us -> none  [the longest x1 128 us: far_part(): lax.all_gather(block_src, 'col', axis=1, tiled=True)]
    reduce_sum x6 -> x0, other arithmetic: 77.4 us -> none  [the longest x4 76.3 us: accumulate(): jnp.sum(kernel_re * values[0][None, :] - kernel_im * values[1][None, :],...]
    pallas_call x0 -> x1, Pallas kernels: none -> 37.7 us  [local(): pl.pallas_call(functools.partial(kernel, n_row, n_col, planes, 1.0 / math...]
    all_gather x2 -> x0, blocking collectives: 15.3 us -> none  [the longest x1 8.85 us: far_part(): lax.all_gather(currents, 'row', axis=1, tiled=True)]
    slice x5 -> x0, local copies, waits for them, and re-layouts: 14.1 us -> none  [the longest x4 14.1 us: accumulate(): values[0][None, :]]
    all_to_all x1 -> x0, starting transfers between devices: 12.6 us -> none  [near_part(): lax.all_to_all(outgoing, 'col', split_axis=0, concat_axis=0, tiled=True)]
    all_to_all x1 -> x0, waiting for transfers between devices: 10.8 us -> none  [near_part(): lax.all_to_all(outgoing, 'col', split_axis=0, concat_axis=0, tiled=True)]
    dot_general x6 -> x0, matrix products: 9.21 us -> none  [the longest x1 1.99 us: near_part(): jnp.einsum('kij,kj->ki', blocks_im, chosen[:, 0], precision=highest)]
  transfers between devices with their start and end apart: 3 -> 0, of which waited for: 3 -> 0; matrix products, arithmetic and copies ran while one was open for 3% -> 0% of each run, Pallas kernels for 0% -> 0%
where the time goes in v1:
time: 41.2 us; the launch traced here: 41 us
  Pallas kernels  37.7 us (92%)
  local copies, waits for them, and re-layouts  3.25 us (8%)
    pallas_call x1, Pallas kernels, local(): pl.pallas_call(functools.partial(kernel, n_row, n_col, planes, 1.0 / math...  37.7 us
    unnamed x13, local copies, waits for them, and re-layouts  3.25 us

profile of v1, /device:TPU:1, one launch (start us, length us, event | category | flops | bytes accessed | tf_op | source)
XLA Modules:
  0.0 41.0 jit_solution(5672286081186253752)
XLA Ops:
  0.0 0.0 copy-start.4
  0.0 0.8 %copy.7.dest_ref = s32[64,1]{1,0:T(8,128)S(1)} copy(s32[64,1]{0,1:T(1,128)} %param.10) | data formatting | bytes 512 | tf_op args[4]
  0.8 0.0 copy-done.4
  0.8 0.0 copy-start.1
  0.8 0.0 copy-start.2
  0.8 0.0 copy-start.3
  0.8 0.1 copy.8.tile_ref
  0.9 0.6 %copy-done.1 = f32[3,1024]{1,0:T(4,128)S(1)} copy-done((f32[3,1024]{1,0:T(4,128)S(1)}, f32[3,1024]{1,0:T(4,128)}, u32[]{:S(2)}) %copy-start.1) | copy-done | bytes 12312
  1.5 0.0 copy-done.2
  1.5 0.0 copy-done.3
  1.5 0.0 copy-start
  1.5 1.2 %copy-done = f32[64,2,16,128]{3,2,1,0:T(8,128)S(1)} copy-done((f32[64,2,16,128]{3,2,1,0:T(8,128)S(1)}, f32[64,2,16,128]{3,2,1,0:T(8,128)}, u32[]{:S(2)}) %copy-start) | copy-done | bytes 1048600
  2.7 37.7 %shard_map.64 = f32[2,16]{1,0:T(2,128)S(1)} custom-call(f32[3,16]{1,0:T(4,128)S(1)} %copy-done.3, f32[3,1024]{1,0:T(4,128)S(1)} %copy-done.1, f32[2,1024]{1,0:T(2,128)S(1)} %copy-done.2, f32[64,2,16,128]{3,2,1,0:T(8,128)S(1)} %copy-done, s32[64,1]{1,0:T(8,128)S(1)} %copy.7.dest_ref, s32[64,1]{1,0:T(8,128)S(1)} %copy.8.tile_ref), custom_call_target="tpu_custom_call" | custom-call | tf_op jit(solution)/shard_map/pallas_call | solution.py:370
  40.4 0.6 %copy.10 = f32[2,16]{1,0:T(2,128)} copy(f32[2,16]{1,0:T(2,128)S(1)} %shard_map.64) | data formatting | bytes 256
Async XLA Ops:
  0.0 0.8 %copy-start.4 = (s32[64,1]{0,1:T(1,128)S(1)}, s32[64,1]{0,1:T(1,128)}, u32[]{:S(2)}) copy-start(s32[64,1]{0,1:T(1,128)} %param.11) | copy-start | bytes 772
  0.8 0.7 %copy-start.1 = (f32[3,1024]{1,0:T(4,128)S(1)}, f32[3,1024]{1,0:T(4,128)}, u32[]{:S(2)}) copy-start(f32[3,1024]{1,0:T(4,128)} %src_ref.1) | copy-start | bytes 36868
  0.8 0.7 %copy-start.2 = (f32[2,1024]{1,0:T(2,128)S(1)}, f32[2,1024]{1,0:T(2,128)}, u32[]{:S(2)}) copy-start(f32[2,1024]{1,0:T(2,128)} %cur_ref.1) | copy-start | bytes 24580
  0.8 0.7 %copy-start.3 = (f32[3,16]{1,0:T(4,128)S(1)}, f32[3,16]{1,0:T(4,128)}, u32[]{:S(2)}) copy-start(f32[3,16]{1,0:T(4,128)} %tp_ref.1) | copy-start | bytes 580
  1.5 1.2 %copy-start = (f32[64,2,16,128]{3,2,1,0:T(8,128)S(1)}, f32[64,2,16,128]{3,2,1,0:T(8,128)}, u32[]{:S(2)}) copy-start(f32[64,2,16,128]{3,2,1,0:T(8,128)} %blocks_hbm.1) | copy-start | bytes 3145732

commit v2 on v1

--- a/solution.py
+++ b/solution.py
@@ -186,16 +186,13 @@
 
     barrier = pltpu.get_barrier_semaphore()
 
-    def greet(k, _):
-        pl.semaphore_signal(barrier, inc=1, device_id=member(k)[1], device_id_type=MESH)
-        return 0
-
-    def greet_level(k, _):
-        pl.semaphore_signal(barrier, inc=1, device_id=level(k)[1], device_id_type=MESH)
-        return 0
-
-    lax.fori_loop(1, planes, greet_level, 0)
-    lax.fori_loop(1, members, greet, 0)
+    def greet(device):
+        pl.semaphore_signal(barrier, inc=1, device_id=device, device_id_type=MESH)
+
+    for k in range(1, members):
+        greet(member(k)[1])
+    for k in range(1, planes):
+        greet(level(k)[1])
 
     points = (tp_ref[...] - 0.5) * TURNS
     repeated = jnp.concatenate([points] * (LANES // width), axis=1)
@@ -221,70 +218,68 @@
 
     prepare(plane, 0)
 
+    pl.semaphore_wait(barrier, members - 1 + planes - 1)
+
+    def target_copy(k):
+        return pltpu.make_async_remote_copy(
+            src_ref=tbuf.at[me], dst_ref=tbuf.at[me], send_sem=tsend_sem,
+            recv_sem=trecv_sem, device_id=member(k)[1], device_id_type=MESH,
+        )
+
+    def source_copy(slot, device):
+        return pltpu.make_async_remote_copy(
+            src_ref=sbuf.at[slot], dst_ref=sbuf.at[slot], send_sem=ssend_sem,
+            recv_sem=srecv_sem.at[slot], device_id=device, device_id_type=MESH,
+        )
+
+    def near_copy(k):
+        other, device = level(k)
+        return pltpu.make_async_remote_copy(
+            src_ref=nsend.at[other], dst_ref=nbuf.at[plane], send_sem=nsend_sem,
+            recv_sem=nrecv_sem, device_id=device, device_id_type=MESH,
+        )
+
+    def result_copy(k):
+        other, device = member(k)
+        return pltpu.make_async_remote_copy(
+            src_ref=rsend.at[other // places], dst_ref=rbuf.at[me], send_sem=rsend_sem,
+            recv_sem=rrecv_sem, device_id=device, device_id_type=MESH,
+        )
+
+    def all_of(buf, count, send_sem, recv_sem):
+        part = buf.at[pl.ds(0, count)]
+        return pltpu.make_async_remote_copy(
+            src_ref=part, dst_ref=part, send_sem=send_sem,
+            recv_sem=recv_sem, device_id=(row, col), device_id_type=MESH,
+        )
+
+    targets = all_of(tbuf, members - 1, tsend_sem, trecv_sem)
+    nears = all_of(nbuf, planes - 1, nsend_sem, nrecv_sem)
+    results = all_of(rbuf, members - 1, rsend_sem, rrecv_sem)
+    sources = all_of(sbuf, planes - 1, ssend_sem, srecv_sem.at[0])
+
+    def offset(i):
+        half = (i + 1) // 2
+        return lax.rem(planes + (2 * lax.rem(i, 2) - 1) * half, planes)
+
+    for k in range(1, members):
+        target_copy(k).start()
+
+    def send_source(i, _):
+        source_copy(plane, level(offset(i))[1]).start()
+        return 0
+
+    lax.fori_loop(1, planes, send_source, 0)
+
     fetch.wait()
     near = near_rows(cur_ref[...], blocks, dest_ref[...], tile_ref[...], planes)
     for k in range(planes):
         nsend[k] = jnp.concatenate([near[k : k + 1], near[planes + k : planes + k + 1]], axis=0)
-
-    pl.semaphore_wait(barrier, members - 1 + planes - 1)
-
-    def target_copy(k):
-        other, device = member(k)
-        return other, lambda slot, sem: pltpu.make_async_remote_copy(
-            src_ref=tbuf.at[slot], dst_ref=tbuf.at[slot], send_sem=tsend_sem.at[other],
-            recv_sem=trecv_sem.at[sem], device_id=device, device_id_type=MESH,
-        )
-
-    def source_copy(k):
-        other, device = level(k)
-        return other, lambda slot, sem: pltpu.make_async_remote_copy(
-            src_ref=sbuf.at[slot], dst_ref=sbuf.at[slot], send_sem=ssend_sem.at[other],
-            recv_sem=srecv_sem.at[sem], device_id=device, device_id_type=MESH,
-        )
-
-    def near_copy(k):
-        other, device = level(k)
-        return other, lambda slot, sem: pltpu.make_async_remote_copy(
-            src_ref=nsend.at[other], dst_ref=nbuf.at[slot], send_sem=nsend_sem.at[other],
-            recv_sem=nrecv_sem.at[sem], device_id=device, device_id_type=MESH,
-        )
-
-    def result_copy(k):
-        other, device = member(k)
-        return other, lambda slot, sem: pltpu.make_async_remote_copy(
-            src_ref=rsend.at[other // places], dst_ref=rbuf.at[slot], send_sem=rsend_sem.at[other],
-            recv_sem=rrecv_sem.at[sem], device_id=device, device_id_type=MESH,
-        )
-
-    def each(copy, count, mine, act):
-        def body(k, _):
-            other, make = copy(k)
-            if act == "start":
-                make(mine, mine).start()
-            elif act == "recv":
-                make(other, other).wait_recv()
-            else:
-                make(mine, mine).wait_send()
-            return 0
-
-        lax.fori_loop(1, count, body, 0)
-
-    def offset(i):
-        half = (i + 1) // 2
-        return lax.rem(planes + (2 * lax.rem(i, 2) - 1) * half, planes)
-
-    each(target_copy, members, me, "start")
-
-    def send_source(i, _):
-        _, make = source_copy(offset(i))
-        make(plane, plane).start()
-        return 0
-
-    lax.fori_loop(1, planes, send_source, 0)
     nbuf[plane] = nsend[plane]
-    each(near_copy, planes, plane, "start")
-
-    each(target_copy, members, me, "recv")
+    for k in range(1, planes):
+        near_copy(k).start()
+
+    targets.wait_recv()
     points = []
     for g in range(n_row):
         joined = tbuf[g * places]
@@ -318,8 +313,8 @@
 
         @pl.when(i < planes - 1)
         def _():
-            other, make = source_copy(offset(ahead))
-            make(other, other).wait_recv()
+            other, device = level(offset(ahead))
+            source_copy(other, device).wait_recv()
 
         slot = lax.rem(i, 2)
         prepare(lax.rem(plane + offset(ahead), planes), 1 - slot)
@@ -337,7 +332,7 @@
     real = jnp.sum((2.0 * S3 * S3) * cosines - total, axis=0, keepdims=True) * unit
     imag = jnp.sum(sines, axis=0, keepdims=True) * (-2.0 * S3 * abs(S3) * unit)
 
-    each(near_copy, planes, plane, "recv")
+    nears.wait_recv()
     near = nbuf[0]
     for k in range(1, planes):
         near = near + nbuf[k]
@@ -346,18 +341,19 @@
         part = part + jnp.where(row == g, 1.0, 0.0) * near
         rsend[g] = part
     rbuf[me] = rsend[row]
-    each(result_copy, members, me, "start")
-    each(target_copy, members, me, "send")
-    each(source_copy, planes, plane, "send")
-    each(near_copy, planes, plane, "send")
-    each(result_copy, members, me, "recv")
+    for k in range(1, members):
+        result_copy(k).start()
+    targets.wait_send()
+    sources.wait_send()
+    nears.wait_send()
+    results.wait_recv()
     field = rbuf[0]
     for k in range(1, members):
         field = field + rbuf[k]
     field = jnp.concatenate([field, jnp.zeros((6, LANES), F32)], axis=0)
     field = pltpu.roll(field, lax.rem(LANES - place * width, LANES), 1)
     out_ref[...] = field[0:2, 0:width]
-    each(result_copy, members, me, "send")
+    results.wait_send()
 
 
 def local(planes, total_sources, test_points, src_points, currents, near_blocks, near_dest, near_tile):
@@ -384,14 +380,14 @@
             pltpu.VMEM((FEATURES, n_tgt + 2 * LANES), BF16),
             pltpu.VMEM((n_src // CHUNK, CHUNK, n_tgt + 2 * LANES), F32),
             dma,
-            dma((members,)),
-            dma((members,)),
+            dma,
+            dma,
+            dma,
             dma((planes,)),
-            dma((planes,)),
-            dma((planes,)),
-            dma((planes,)),
-            dma((members,)),
-            dma((members,)),
+            dma,
+            dma,
+            dma,
+            dma,
         ],
         compiler_params=pltpu.CompilerParams(collective_id=0, has_side_effects=True, vmem_limit_bytes=48 << 20),
     )(test_points, src_points, currents, near_blocks, near_dest, near_tile)

time: 41.2 us -> 39.5 us (0.959)
  Pallas kernels: 37.7 us -> 36 us
    pallas_call x1, Pallas kernels: 37.7 us -> 36 us  [local(): pl.pallas_call(functools.partial(kernel, n_row, n_col, planes, 1.0 / math...]
where the time goes in v2:
time: 39.5 us; the launch traced here: 39.3 us
  Pallas kernels  36 us (91%)
  local copies, waits for them, and re-layouts  3.25 us (8%)
    pallas_call x1, Pallas kernels, local(): pl.pallas_call(functools.partial(kernel, n_row, n_col, planes, 1.0 / math...  36 us
    unnamed x13, local copies, waits for them, and re-layouts  3.25 us

profile of v2, /device:TPU:1, one launch (start us, length us, event | category | flops | bytes accessed | tf_op | source)
XLA Modules:
  0.0 39.3 jit_solution(585359322966923290)
XLA Ops:
  0.0 0.0 copy-start.4
  0.0 0.8 %copy.7.dest_ref = s32[64,1]{1,0:T(8,128)S(1)} copy(s32[64,1]{0,1:T(1,128)} %param.10) | data formatting | bytes 512 | tf_op args[4]
  0.8 0.0 copy-done.4
  0.8 0.0 copy-start.1
  0.8 0.0 copy-start.2
  0.8 0.0 copy-start.3
  0.8 0.1 copy.8.tile_ref
  0.9 0.6 %copy-done.1 = f32[3,1024]{1,0:T(4,128)S(1)} copy-done((f32[3,1024]{1,0:T(4,128)S(1)}, f32[3,1024]{1,0:T(4,128)}, u32[]{:S(2)}) %copy-start.1) | copy-done | bytes 12312
  1.5 0.0 copy-done.2
  1.5 0.0 copy-done.3
  1.5 0.0 copy-start
  1.5 1.2 %copy-done = f32[64,2,16,128]{3,2,1,0:T(8,128)S(1)} copy-done((f32[64,2,16,128]{3,2,1,0:T(8,128)S(1)}, f32[64,2,16,128]{3,2,1,0:T(8,128)}, u32[]{:S(2)}) %copy-start) | copy-done | bytes 1048600
  2.7 36.0 %shard_map.64 = f32[2,16]{1,0:T(2,128)S(1)} custom-call(f32[3,16]{1,0:T(4,128)S(1)} %copy-done.3, f32[3,1024]{1,0:T(4,128)S(1)} %copy-done.1, f32[2,1024]{1,0:T(2,128)S(1)} %copy-done.2, f32[64,2,16,128]{3,2,1,0:T(8,128)S(1)} %copy-done, s32[64,1]{1,0:T(8,128)S(1)} %copy.7.dest_ref, s32[64,1]{1,0:T(8,128)S(1)} %copy.8.tile_ref), custom_call_target="tpu_custom_call" | custom-call | tf_op jit(solution)/shard_map/pallas_call | solution.py:366
  38.8 0.6 %copy.10 = f32[2,16]{1,0:T(2,128)} copy(f32[2,16]{1,0:T(2,128)S(1)} %shard_map.64) | data formatting | bytes 256
Async XLA Ops:
  0.0 0.8 %copy-start.4 = (s32[64,1]{0,1:T(1,128)S(1)}, s32[64,1]{0,1:T(1,128)}, u32[]{:S(2)}) copy-start(s32[64,1]{0,1:T(1,128)} %param.11) | copy-start | bytes 772
  0.8 0.7 %copy-start.1 = (f32[3,1024]{1,0:T(4,128)S(1)}, f32[3,1024]{1,0:T(4,128)}, u32[]{:S(2)}) copy-start(f32[3,1024]{1,0:T(4,128)} %src_ref.1) | copy-start | bytes 36868
  0.8 0.7 %copy-start.2 = (f32[2,1024]{1,0:T(2,128)S(1)}, f32[2,1024]{1,0:T(2,128)}, u32[]{:S(2)}) copy-start(f32[2,1024]{1,0:T(2,128)} %cur_ref.1) | copy-start | bytes 24580
  0.8 0.7 %copy-start.3 = (f32[3,16]{1,0:T(4,128)S(1)}, f32[3,16]{1,0:T(4,128)}, u32[]{:S(2)}) copy-start(f32[3,16]{1,0:T(4,128)} %tp_ref.1) | copy-start | bytes 580
  1.5 1.2 %copy-start = (f32[64,2,16,128]{3,2,1,0:T(8,128)S(1)}, f32[64,2,16,128]{3,2,1,0:T(8,128)}, u32[]{:S(2)}) copy-start(f32[64,2,16,128]{3,2,1,0:T(8,128)} %blocks_hbm.1) | copy-start | bytes 3145732

commit v3 on v2

--- a/solution.py
+++ b/solution.py
@@ -141,13 +141,13 @@
     spread = (
         lax.broadcasted_iota(jnp.int32, (items, n), 1) // width == lax.broadcasted_iota(jnp.int32, (items, n), 0)
     ).astype(F32)
-    along = lambda v, k: dot(jnp.broadcast_to(v.astype(F32), (items, k)), spread, 0, 0)
+    along = lambda v, k: dot(jnp.broadcast_to(v.astype(F32), (k, items)), spread, 1, 0)
     mine = along(tile, tiles) == lax.broadcasted_iota(jnp.int32, (tiles, n), 0).astype(F32)
     real = jnp.sum(jnp.where(mine, real, 0.0), axis=0, keepdims=True)
     imag = jnp.sum(jnp.where(mine, imag, 0.0), axis=0, keepdims=True)
     plane = along(dest % planes, planes) == lax.broadcasted_iota(jnp.int32, (planes, n), 0).astype(F32)
     left = jnp.concatenate([jnp.where(plane, real, 0.0), jnp.where(plane, imag, 0.0)], axis=0)
-    place = dot(spread, jnp.broadcast_to((dest // planes).astype(F32), (items, LANES)), 0, 0)
+    place = dot(spread, jnp.broadcast_to((dest // planes).astype(F32), (LANES, items)), 0, 1)
     lane = lax.broadcasted_iota(jnp.int32, (n, LANES), 1)
     row = lax.broadcasted_iota(jnp.int32, (n, LANES), 0)
     right = jnp.where((lane % width == row % width) & (place == (lane // width).astype(F32)), 1.0, 0.0)
@@ -160,8 +160,8 @@
 
 def kernel(
     n_row, n_col, planes, scale,
-    tp_ref, src_ref, cur_ref, blocks_hbm, dest_ref, tile_ref, out_ref,
-    tbuf, sbuf, nbuf, nsend, rbuf, rsend, blocks, fa, fb, q_ref,
+    tp_hbm, src_hbm, cur_hbm, blocks_hbm, dest_hbm, tile_hbm, out_ref,
+    tp_ref, src_ref, cur_ref, dest_ref, tile_ref, tbuf, sbuf, nbuf, nsend, rbuf, rsend, blocks, fa, fb, q_ref,
     copy_sem, tsend_sem, trecv_sem, ssend_sem, srecv_sem, nsend_sem, nrecv_sem, rsend_sem, rrecv_sem,
 ):
     places = n_col // planes
@@ -173,8 +173,15 @@
     place, plane = col // planes, col % planes
     me = row * places + place
 
-    fetch = pltpu.make_async_copy(blocks_hbm, blocks, copy_sem)
-    fetch.start()
+    fetches = [
+        pltpu.make_async_copy(a, b, copy_sem.at[i])
+        for i, (a, b) in enumerate((
+            (tp_hbm, tp_ref), (cur_hbm, cur_ref), (src_hbm, src_ref),
+            (dest_hbm, dest_ref), (tile_hbm, tile_ref), (blocks_hbm, blocks),
+        ))
+    ]
+    for fetch in fetches:
+        fetch.start()
 
     def member(k):
         other = lax.rem(me + k, members)
@@ -193,6 +200,15 @@
         greet(member(k)[1])
     for k in range(1, planes):
         greet(level(k)[1])
+
+    for i in range(FEATURES // 8):
+        fb[pl.ds(i * 8, 8), :] = jnp.zeros((8, n_tgt + 2 * LANES), BF16)
+    index = lax.broadcasted_iota(jnp.int32, (16, LANES), 0)
+    fb[pl.ds(64, 16), pl.ds(n_tgt, LANES)] = jnp.where(index < 3, 1.0, 0.0).astype(BF16)
+    fb[pl.ds(64, 16), pl.ds(n_tgt + LANES, LANES)] = jnp.where((index >= 3) & (index < 6), 1.0, 0.0).astype(BF16)
+
+    for fetch in fetches[:3]:
+        fetch.wait()
 
     points = (tp_ref[...] - 0.5) * TURNS
     repeated = jnp.concatenate([points] * (LANES // width), axis=1)
@@ -205,12 +221,6 @@
         [(src_ref[...] - 0.5) * TURNS, size, angle, jnp.zeros((3, n_src), F32)], axis=0
     )
 
-    for i in range(FEATURES // 8):
-        fb[pl.ds(i * 8, 8), :] = jnp.zeros((8, n_tgt + 2 * LANES), BF16)
-    index = lax.broadcasted_iota(jnp.int32, (16, LANES), 0)
-    fb[pl.ds(64, 16), pl.ds(n_tgt, LANES)] = jnp.where(index < 3, 1.0, 0.0).astype(BF16)
-    fb[pl.ds(64, 16), pl.ds(n_tgt + LANES, LANES)] = jnp.where((index >= 3) & (index < 6), 1.0, 0.0).astype(BF16)
-
     def prepare(which, slot):
         groups = source_features(sbuf[which])
         for i in range(0, len(groups), 2):
@@ -271,7 +281,8 @@
 
     lax.fori_loop(1, planes, send_source, 0)
 
-    fetch.wait()
+    for fetch in fetches[3:]:
+        fetch.wait()
     near = near_rows(cur_ref[...], blocks, dest_ref[...], tile_ref[...], planes)
     for k in range(planes):
         nsend[k] = jnp.concatenate([near[k : k + 1], near[planes + k : planes + k + 1]], axis=0)
@@ -366,9 +377,14 @@
     return pl.pallas_call(
         functools.partial(kernel, n_row, n_col, planes, 1.0 / math.sqrt(total_sources)),
         out_shape=jax.ShapeDtypeStruct((2, test_points.shape[1]), F32),
-        in_specs=[vmem, vmem, vmem, pl.BlockSpec(memory_space=pl.ANY), vmem, vmem],
+        in_specs=[pl.BlockSpec(memory_space=pltpu.HBM)] * 6,
         out_specs=vmem,
         scratch_shapes=[
+            pltpu.VMEM(test_points.shape, F32),
+            pltpu.VMEM(src_points.shape, F32),
+            pltpu.VMEM(currents.shape, F32),
+            pltpu.VMEM((1, near_dest.shape[0]), jnp.int32),
+            pltpu.VMEM((1, near_tile.shape[0]), jnp.int32),
             pltpu.VMEM((members, 4, LANES), F32),
             pltpu.VMEM((planes, 8, n_src), F32),
             pltpu.VMEM((planes, 2, LANES), F32),
@@ -379,7 +395,7 @@
             pltpu.VMEM((2, FEATURES, n_src), BF16),
             pltpu.VMEM((FEATURES, n_tgt + 2 * LANES), BF16),
             pltpu.VMEM((n_src // CHUNK, CHUNK, n_tgt + 2 * LANES), F32),
-            dma,
+            dma((6,)),
             dma,
             dma,
             dma,
@@ -389,8 +405,8 @@
             dma,
             dma,
         ],
-        compiler_params=pltpu.CompilerParams(collective_id=0, has_side_effects=True, vmem_limit_bytes=48 << 20),
-    )(test_points, src_points, currents, near_blocks, near_dest, near_tile)
+        compiler_params=pltpu.CompilerParams(collective_id=0, has_side_effects=True, vmem_limit_bytes=67_043_328),
+    )(test_points, src_points, currents, near_blocks, near_dest.reshape(1, -1), near_tile.reshape(1, -1))
 
 
 def solution(mesh):

time: 39.5 us -> 38 us (0.962)
  local copies, waits for them, and re-layouts: 3.25 us -> 1.24 us
  Pallas kernels: 36 us -> 36.6 us
    unnamed x13 -> x1, local copies, waits for them, and re-layouts: 3.25 us -> 1.24 us
    pallas_call x1, Pallas kernels: 36 us -> 36.6 us  [local(): pl.pallas_call(functools.partial(kernel, n_row, n_col, planes, 1.0 / math...]
where the time goes in v3:
time: 38 us; the launch traced here: 37.8 us
  Pallas kernels  36.6 us (96%)
  local copies, waits for them, and re-layouts  1.24 us (3%)
    pallas_call x1, Pallas kernels, local(): pl.pallas_call(functools.partial(kernel, n_row, n_col, planes, 1.0 / math...  36.6 us
    unnamed x1, local copies, waits for them, and re-layouts  1.24 us

profile of v3, /device:TPU:1, one launch (start us, length us, event | category | flops | bytes accessed | tf_op | source)
XLA Modules:
  0.0 37.8 jit_solution(11082286862032966145)
XLA Ops:
  0.0 36.6 %shard_map.64 = f32[2,16]{1,0:T(2,128)} custom-call(f32[3,16]{1,0:T(4,128)} %tp_hbm.1, f32[3,1024]{1,0:T(4,128)} %src_hbm.1, f32[2,1024]{1,0:T(2,128)} %cur_hbm.1, f32[64,2,16,128]{3,2,1,0:T(8,128)} %blocks_hbm.1, s32[1,64]{1,0:T(1,128)} %bitcast.2, s32[1,64]{1,0:T(1,128)} %bitcast.3), custom_call_target="tpu_custom_call" | custom-call | tf_op jit(solution)/shard_map/pallas_call | solution.py:377
  36.6 1.2 %copy.8 = f32[2,16]{1,0:T(2,128)} copy(f32[2,16]{1,0:T(2,128)} %shard_map.64) | data formatting | bytes 256
